TPU v7x, 128 devices: a whole 4x4x4 slice. The times are simulated.
128 devices in a mesh: node: 4 (over y_hi, core), hst: 32 (over y_lo, x, z).
Axes of the slice: x: 4, y: 4 (y_hi: 2, y_lo: 2; y = y_hi * 2 + y_lo), z: 4, core: 2. Of those that a mesh axis runs over, the one named last changes fastest.
Arguments:
- hidden: bfloat16 [32, 4096, 640], P('hst', 'node'), may hold values from -6 to 6
- cotangent: bfloat16 [32, 4096, 4608], P('hst', 'node'), may hold values from -12 to 12
- anchor: float32 [32, 640, 4608], P('hst', 'node'), may hold values from -0.25 to 0.25
- momentum: float32 [32, 640, 4608], P('hst', 'node'), may hold values from -0.6 to 0.6
- round_mask: int32 [1], replicated, may hold values from 1 to 31
Outputs:
- weights_out: bfloat16 [32, 640, 4608], P('hst')
- momentum_out: float32 [32, 640, 4608], P('hst', 'node')
Inputs may be any that keep to these rules, and one draw needn't show every extreme that they name: round_mask is the same for all hosts; host i averages with the hosts i XOR s for every s whose bits lie within round_mask.
All inputs are finite; a program needn't handle non-finite values.
Results may differ from a plain program's by a relative error of at most 0.009.
Values may be sent and summed in bfloat16 or wider, within the bound.
A program may use at most 256 MiB of HBM per device.

v0:
```python
import jax
import jax.numpy as jnp
from jax import lax
from jax.sharding import PartitionSpec as P

base_rate = 0.5
slow_rate = 1.0
slow_beta = 0.7


def swapped(block, axis, bit):
    count = lax.axis_size(axis)
    route = []
    for low in range(count):
        high = low | 1 << bit
        if high != low and high < count:
            route += [(low, high), (high, low)]
    return lax.ppermute(block, axis, route)


def half_step(current, bit_index):
    other_rows = swapped(current.astype(jnp.bfloat16), "hst", bit_index).astype(current.dtype)
    return 0.5 * (current + other_rows)


def local(hidden, cotangent, anchor, momentum, round_mask):
    tokens_here = hidden[0]
    grads_in = cotangent[0]
    token_scale = 1.0 / (tokens_here.shape[0] * lax.axis_size("node"))
    product = lax.dot_general(
        tokens_here, grads_in, (((0,), (0,)), ((), ())), preferred_element_type=jnp.float32
    )
    gradient = lax.psum_scatter(
        (product * token_scale).astype(jnp.bfloat16), "node", scatter_dimension=0, tiled=True
    ).astype(jnp.float32)
    stepped = anchor[0] - base_rate * gradient
    mask_value = round_mask[0]
    host_count = lax.axis_size("hst")
    bit_count = host_count.bit_length() - 1
    bit_list = list(range(bit_count))
    averaged = stepped
    for bit_index in bit_list:
        active = jnp.bitwise_and(jnp.right_shift(mask_value, bit_index), 1) == 1
        averaged = jnp.where(active, half_step(averaged, bit_index), averaged)
    momentum_new = slow_beta * momentum[0] + (anchor[0] - averaged) / base_rate
    updated = (anchor[0] - slow_rate * base_rate * momentum_new).astype(jnp.bfloat16)
    weights_whole = lax.all_gather(updated[None], "node", axis=1, tiled=True)
    return (weights_whole, momentum_new[None])


def solution(mesh):
    placed = (
        P("hst", "node", None),
        P("hst", "node", None),
        P("hst", "node", None),
        P("hst", "node", None),
        P(),
    )
    return jax.shard_map(
        local,
        mesh=mesh,
        in_specs=placed,
        out_specs=(P("hst", None, None), P("hst", "node", None)),
        check_vma=False,
    )
```

profile of v0, /device:TPU:1, one launch (start us, length us, event | category | flops | bytes accessed | tf_op | source)
XLA Modules:
  0.0 318.9 jit_solution(657283550039399668)
XLA Ops:
  7.2 0.0 copy-start
  7.2 0.0 reduce-scatter.2.cloned.1.call-start
  7.2 1.3 copy-done
  8.5 10.5 %multiply_convert_fusion = bf16[640,4608]{1,0:T(8,128)(2,1)} fusion(bf16[1,1024,4608]{2,1,0:T(8,128)(2,1)} %param.6, bf16[1,1024,640]{2,1,0:T(8,128)(2,1)S(1)} %copy-done), kind=kOutput, calls=%fused_computation | convolution fusion | flops 6045696000 | bytes 16646144 | tf_op jit(solution)/shard_map/dot_general | solution.py:30
  19.0 0.0 reduce-scatter.2.cloned.1.call-update
  19.0 0.0 all-gather.3.cloned.1.call-start
  19.0 66.0 %reduce-scatter.2.cloned.1.call-done = bf16[160,4608]{1,0:T(8,128)(2,1)} async-done(((bf16[640,4608]{1,0:T(8,128)(2,1)}), bf16[160,4608]{1,0:T(8,128)(2,1)}) %reduce-scatter.2.cloned.1.call-update) | async-done | bytes 1474576 | tf_op jit(solution)/shard_map/reduce_scatter | solution.py:33
  85.0 0.0 copy-start.1
  85.0 0.0 copy-start.2
  85.0 2.8 fusion.6
  87.8 1.3 collective-permute-start
  89.8 31.2 %collective-permute-done = bf16[160,4608]{1,0:T(8,128)(2,1)S(1)} collective-permute-done((bf16[160,4608]{1,0:T(8,128)(2,1)S(1)}, bf16[160,4608]{1,0:T(8,128)(2,1)S(1)}, u32[]{:S(2)}, u32[]{:S(2)}) %collective-permute-start) | collective-permute-done | bytes 1474592 | tf_op jit(solution)/shard_map/ppermute | solution.py:18
  121.1 0.0 copy-done.1
  121.1 0.0 copy-done.2
  121.1 0.7 fusion.11
  121.8 2.9 collective-permute-start.1
  124.7 30.9 %collective-permute-done.1 = bf16[160,4608]{1,0:T(8,128)(2,1)S(1)} collective-permute-done((bf16[160,4608]{1,0:T(8,128)(2,1)S(1)}, bf16[160,4608]{1,0:T(8,128)(2,1)S(1)}, u32[]{:S(2)}, u32[]{:S(2)}) %collective-permute-start.1) | collective-permute-done | bytes 1474592 | tf_op jit(solution)/shard_map/ppermute | solution.py:18
  155.6 0.4 fusion.7
  156.0 1.2 collective-permute-start.2
  157.3 30.2 %collective-permute-done.2 = bf16[160,4608]{1,0:T(8,128)(2,1)S(1)} collective-permute-done((bf16[160,4608]{1,0:T(8,128)(2,1)S(1)}, bf16[160,4608]{1,0:T(8,128)(2,1)S(1)}, u32[]{:S(2)}, u32[]{:S(2)}) %collective-permute-start.2) | collective-permute-done | bytes 1474592 | tf_op jit(solution)/shard_map/ppermute | solution.py:18
  187.4 0.8 fusion.10
  188.3 2.7 collective-permute-start.3
  191.0 29.2 %collective-permute-done.3 = bf16[160,4608]{1,0:T(8,128)(2,1)S(1)} collective-permute-done((bf16[160,4608]{1,0:T(8,128)(2,1)S(1)}, bf16[160,4608]{1,0:T(8,128)(2,1)S(1)}, u32[]{:S(2)}, u32[]{:S(2)}) %collective-permute-start.3) | collective-permute-done | bytes 1474592 | tf_op jit(solution)/shard_map/ppermute | solution.py:18
  220.2 0.0 copy-start.3
  220.2 0.4 fusion.8
  220.7 0.3 collective-permute-start.4
  221.0 29.2 %collective-permute-done.4 = bf16[160,4608]{1,0:T(8,128)(2,1)S(1)} collective-permute-done((bf16[160,4608]{1,0:T(8,128)(2,1)S(1)}, bf16[160,4608]{1,0:T(8,128)(2,1)S(1)}, u32[]{:S(2)}, u32[]{:S(2)}) %collective-permute-start.4) | collective-permute-done | bytes 1474592 | tf_op jit(solution)/shard_map/ppermute | solution.py:18
  250.2 0.0 copy-done.3
  250.2 3.5 %fusion.5 = (bf16[160,4608]{1,0:T(8,128)(2,1)}, f32[160,4608]{1,0:T(8,128)}) fusion(f32[1,160,4608]{2,1,0:T(8,128)S(1)} %copy-done.1, bf16[160,4608]{1,0:T(8,128)(2,1)S(1)} %collective-permute-done.4, f32[160,4608]{1,0:T(8,128)S(1)} %get-tuple-element.5, bf16[160,4608]{1,0:T(8,128)(2,1)S(1)} %collective-permute-done.3, pred[]{:T(512)} %bitcast.3, ...), kind=kLoop, calls=%fused_computation.8 | loop fusion | flops 11059200 | bytes 16220162 | tf_op jit(solution)/shard_map/convert_element_type | solution.py:46
  253.7 0.0 all-gather.3.cloned.1.call-update
  253.7 52.7 %all-gather.3.cloned.1.call-done = bf16[640,4608]{1,0:T(8,128)(2,1)} async-done(((bf16[160,4608]{1,0:T(8,128)(2,1)}), bf16[640,4608]{1,0:T(8,128)(2,1)}) %all-gather.3.cloned.1.call-update) | async-done | bytes 5898256 | tf_op jit(solution)/shard_map/all_gather | solution.py:47
  306.4 5.6 %copy.9 = bf16[1,640,4608]{2,1,0:T(8,128)(2,1)} copy(bf16[1,640,4608]{2,1,0:T(8,128)(2,1)} %bitcast.34) | data formatting | bytes 11796480
Async XLA Ops:
  7.2 1.3 copy-start
  7.2 77.9 %reduce-scatter.2.cloned.1.call-start = ((), (), s32[]{:S(2)}) async-start(), calls=%async_computation.1 | async-start | bytes 7372800 | tf_op jit(solution)/shard_map/reduce_scatter | solution.py:33
  19.0 287.4 %all-gather.3.cloned.1.call-start = ((), (), s32[]{:S(2)}) async-start(), calls=%async_computation.2 | async-start | bytes 7372800 | tf_op jit(solution)/shard_map/all_gather | solution.py:47
  85.0 36.0 %copy-start.1 = (f32[1,160,4608]{2,1,0:T(8,128)S(1)}, f32[1,160,4608]{2,1,0:T(8,128)}, u32[]{:S(2)}) copy-start(f32[1,160,4608]{2,1,0:T(8,128)} %param.7) | copy-start | bytes 8847364
  85.0 36.0 %copy-start.2 = (bf16[160,4608]{1,0:T(8,128)(2,1)S(1)}, bf16[160,4608]{1,0:T(8,128)(2,1)}, u32[]{:S(2)}) copy-start(bf16[160,4608]{1,0:T(8,128)(2,1)} %reduce-scatter.2.cloned.1.call-done) | copy-start | bytes 4423684
  87.8 33.2 %collective-permute-start = (bf16[160,4608]{1,0:T(8,128)(2,1)S(1)}, bf16[160,4608]{1,0:T(8,128)(2,1)S(1)}, u32[]{:S(2)}, u32[]{:S(2)}) collective-permute-start(bf16[160,4608]{1,0:T(8,128)(2,1)S(1)} %fusion.6), channel_id=1, source_target_pairs={{0,1},{1,0},{2,3},{3,2},{4,5},{5,4},{6,7},{7,6},{8,9},{9,8},{10,11... | collective-permute-start | bytes 4423688 | tf_op jit(solution)/shard_map/ppermute | solution.py:18
  121.8 33.8 %collective-permute-start.1 = (bf16[160,4608]{1,0:T(8,128)(2,1)S(1)}, bf16[160,4608]{1,0:T(8,128)(2,1)S(1)}, u32[]{:S(2)}, u32[]{:S(2)}) collective-permute-start(bf16[160,4608]{1,0:T(8,128)(2,1)S(1)} %get-tuple-element.6), channel_id=1, source_target_pairs={{0,2},{2,0},{1,3},{3,1},{4,6},{6,4},{5,7},{7,5},{8,10},{10,8},{9,1... | collective-permute-start | bytes 4423688 | tf_op jit(solution)/shard_map/ppermute | solution.py:18
  156.0 31.4 %collective-permute-start.2 = (bf16[160,4608]{1,0:T(8,128)(2,1)S(1)}, bf16[160,4608]{1,0:T(8,128)(2,1)S(1)}, u32[]{:S(2)}, u32[]{:S(2)}) collective-permute-start(bf16[160,4608]{1,0:T(8,128)(2,1)S(1)} %fusion.7), channel_id=1, source_target_pairs={{0,4},{4,0},{1,5},{5,1},{2,6},{6,2},{3,7},{7,3},{8,12},{12,8},{9,1... | collective-permute-start | bytes 4423688 | tf_op jit(solution)/shard_map/ppermute | solution.py:18
  188.3 32.0 %collective-permute-start.3 = (bf16[160,4608]{1,0:T(8,128)(2,1)S(1)}, bf16[160,4608]{1,0:T(8,128)(2,1)S(1)}, u32[]{:S(2)}, u32[]{:S(2)}) collective-permute-start(bf16[160,4608]{1,0:T(8,128)(2,1)S(1)} %get-tuple-element.4), channel_id=1, source_target_pairs={{0,8},{8,0},{1,9},{9,1},{2,10},{10,2},{3,11},{11,3},{4,12},{12,4},... | collective-permute-start | bytes 4423688 | tf_op jit(solution)/shard_map/ppermute | solution.py:18
  220.2 30.0 %copy-start.3 = (f32[1,160,4608]{2,1,0:T(8,128)S(1)}, f32[1,160,4608]{2,1,0:T(8,128)}, u32[]{:S(2)}) copy-start(f32[1,160,4608]{2,1,0:T(8,128)} %param.8) | copy-start | bytes 8847364
  220.7 29.6 %collective-permute-start.4 = (bf16[160,4608]{1,0:T(8,128)(2,1)S(1)}, bf16[160,4608]{1,0:T(8,128)(2,1)S(1)}, u32[]{:S(2)}, u32[]{:S(2)}) collective-permute-start(bf16[160,4608]{1,0:T(8,128)(2,1)S(1)} %fusion.8), channel_id=1, source_target_pairs={{0,16},{16,0},{1,17},{17,1},{2,18},{18,2},{3,19},{19,3},{4,20},{20... | collective-permute-start | bytes 4423688 | tf_op jit(solution)/shard_map/ppermute | solution.py:18
Sparse Core Ops, SparseCore 0:
  19.1 65.8 reduce-scatter.1
  253.8 52.5 all-gather.2
where the time goes:
time: 319 us
  waiting for transfers between devices  269 us (84%)
  between operations  14.7 us (5%)
  matrix products  10.5 us (3%)
  starting transfers between devices  8.68 us (3%)
  other arithmetic  8.62 us (3%)
  local copies, waits for them, and re-layouts  6.9 us (2%)
    ppermute x5, waiting for transfers between devices, swapped(): return lax.ppermute(block, axis, route)  151 us
    reduce_scatter x1, waiting for transfers between devices, local(): lax.psum_scatter((product * token_scale).astype(jnp.bfloat16), 'node', sc...  66 us
    all_gather x1, waiting for transfers between devices, local(): weights_whole = lax.all_gather(updated[None], 'node', axis=1, tiled=True)  52.7 us
    dot_general x1, matrix products, local(): lax.dot_general(tokens_here, grads_in, (((0,), (0,)), ((), ())), preferre...  10.5 us
    ppermute x5, starting transfers between devices, swapped(): return lax.ppermute(block, axis, route)  8.6 us
    unnamed x9, local copies, waits for them, and re-layouts  6.9 us
  transfers between devices with their start and end apart: 7, of which 7 were waited for; matrix products, arithmetic and copies ran while one was open for 0% of the time, Pallas kernels for 0%

commit v1 on v0

--- a/solution.py
+++ b/solution.py
@@ -44,7 +44,9 @@
         averaged = jnp.where(active, half_step(averaged, bit_index), averaged)
     momentum_new = slow_beta * momentum[0] + (anchor[0] - averaged) / base_rate
     updated = (anchor[0] - slow_rate * base_rate * momentum_new).astype(jnp.bfloat16)
-    weights_whole = lax.all_gather(updated[None], "node", axis=1, tiled=True)
+    weights_whole = jnp.concatenate(
+        lax.all_to_all(jnp.stack([updated[None]] * lax.axis_size("node")), "node", 0, 0), axis=1
+    )
     return (weights_whole, momentum_new[None])
 
 

time: 319 us -> 338 us (1.060)
  blocking collectives: 0 us -> 74.8 us
  waiting for transfers between devices: 269 us -> 217 us
    all_to_all x0 -> x1, blocking collectives: none -> 74.8 us  [local(): lax.all_to_all(jnp.stack([updated[None]] * lax.axis_size('node')), 'node'...]
    all_gather x1 -> x0, waiting for transfers between devices: 52.7 us -> none  [local(): weights_whole = lax.all_gather(updated[None], 'node', axis=1, tiled=True)]
  transfers between devices with their start and end apart: 7 -> 6, of which waited for: 7 -> 6; matrix products, arithmetic and copies ran while one was open for 0% -> 0% of each run, Pallas kernels for 0% -> 0%
where the time goes in v1:
time: 338 us
  waiting for transfers between devices  217 us (64%)
  blocking collectives  74.8 us (22%)
  between operations  14.7 us (4%)
  matrix products  10.5 us (3%)
  starting transfers between devices  8.64 us (3%)
  other arithmetic  8.14 us (2%)
  local copies, waits for them, and re-layouts  4.32 us (1%)
    ppermute x5, waiting for transfers between devices, swapped(): return lax.ppermute(block, axis, route)  151 us
    all_to_all x1, blocking collectives, local(): lax.all_to_all(jnp.stack([updated[None]] * lax.axis_size('node')), 'node'...  74.8 us
    reduce_scatter x1, waiting for transfers between devices, local(): lax.psum_scatter((product * token_scale).astype(jnp.bfloat16), 'node', sc...  66 us
    dot_general x1, matrix products, local(): lax.dot_general(tokens_here, grads_in, (((0,), (0,)), ((), ())), preferre...  10.5 us
    ppermute x5, starting transfers between devices, swapped(): return lax.ppermute(block, axis, route)  8.6 us
  transfers between devices with their start and end apart: 6, of which 6 were waited for; matrix products, arithmetic and copies ran while one was open for 0% of the time, Pallas kernels for 0%

profile of v1, /device:TPU:1, one launch (start us, length us, event | category | flops | bytes accessed | tf_op | source)
XLA Modules:
  0.0 337.9 jit_solution(8404988346136414491)
XLA Ops:
  7.2 0.0 copy-start
  7.2 0.0 reduce-scatter.2.cloned.1.call-start
  7.2 1.3 copy-done
  8.5 10.5 %multiply_convert_fusion = bf16[640,4608]{1,0:T(8,128)(2,1)} fusion(bf16[1,1024,4608]{2,1,0:T(8,128)(2,1)} %param.6, bf16[1,1024,640]{2,1,0:T(8,128)(2,1)S(1)} %copy-done), kind=kOutput, calls=%fused_computation | convolution fusion | flops 6045696000 | bytes 16646144 | tf_op jit(solution)/shard_map/dot_general | solution.py:30
  19.0 0.0 reduce-scatter.2.cloned.1.call-update
  19.0 66.0 %reduce-scatter.2.cloned.1.call-done = bf16[160,4608]{1,0:T(8,128)(2,1)} async-done(((bf16[640,4608]{1,0:T(8,128)(2,1)}), bf16[160,4608]{1,0:T(8,128)(2,1)}) %reduce-scatter.2.cloned.1.call-update) | async-done | bytes 1474576 | tf_op jit(solution)/shard_map/reduce_scatter | solution.py:33
  85.0 0.0 copy-start.1
  85.0 0.0 copy-start.2
  85.0 2.8 fusion.6
  87.8 1.3 collective-permute-start
  89.8 31.2 %collective-permute-done = bf16[160,4608]{1,0:T(8,128)(2,1)S(1)} collective-permute-done((bf16[160,4608]{1,0:T(8,128)(2,1)S(1)}, bf16[160,4608]{1,0:T(8,128)(2,1)S(1)}, u32[]{:S(2)}, u32[]{:S(2)}) %collective-permute-start) | collective-permute-done | bytes 1474592 | tf_op jit(solution)/shard_map/ppermute | solution.py:18
  121.1 0.0 copy-done.1
  121.1 0.0 copy-done.2
  121.1 0.7 fusion.11
  121.8 2.9 collective-permute-start.1
  124.7 30.9 %collective-permute-done.1 = bf16[160,4608]{1,0:T(8,128)(2,1)S(1)} collective-permute-done((bf16[160,4608]{1,0:T(8,128)(2,1)S(1)}, bf16[160,4608]{1,0:T(8,128)(2,1)S(1)}, u32[]{:S(2)}, u32[]{:S(2)}) %collective-permute-start.1) | collective-permute-done | bytes 1474592 | tf_op jit(solution)/shard_map/ppermute | solution.py:18
  155.6 0.4 fusion.7
  156.0 1.2 collective-permute-start.2
  157.3 30.2 %collective-permute-done.2 = bf16[160,4608]{1,0:T(8,128)(2,1)S(1)} collective-permute-done((bf16[160,4608]{1,0:T(8,128)(2,1)S(1)}, bf16[160,4608]{1,0:T(8,128)(2,1)S(1)}, u32[]{:S(2)}, u32[]{:S(2)}) %collective-permute-start.2) | collective-permute-done | bytes 1474592 | tf_op jit(solution)/shard_map/ppermute | solution.py:18
  187.4 0.8 fusion.10
  188.3 2.7 collective-permute-start.3
  191.0 29.2 %collective-permute-done.3 = bf16[160,4608]{1,0:T(8,128)(2,1)S(1)} collective-permute-done((bf16[160,4608]{1,0:T(8,128)(2,1)S(1)}, bf16[160,4608]{1,0:T(8,128)(2,1)S(1)}, u32[]{:S(2)}, u32[]{:S(2)}) %collective-permute-start.3) | collective-permute-done | bytes 1474592 | tf_op jit(solution)/shard_map/ppermute | solution.py:18
  220.2 0.0 copy-start.3
  220.2 0.4 fusion.8
  220.7 0.3 collective-permute-start.4
  221.0 29.2 %collective-permute-done.4 = bf16[160,4608]{1,0:T(8,128)(2,1)S(1)} collective-permute-done((bf16[160,4608]{1,0:T(8,128)(2,1)S(1)}, bf16[160,4608]{1,0:T(8,128)(2,1)S(1)}, u32[]{:S(2)}, u32[]{:S(2)}) %collective-permute-start.4) | collective-permute-done | bytes 1474592 | tf_op jit(solution)/shard_map/ppermute | solution.py:18
  250.2 0.0 copy-done.3
  250.2 3.0 fusion.5
  253.2 0.5 stack.3
  253.7 74.8 %all_to_all.5 = bf16[4,1,160,4608]{3,2,1,0:T(8,128)(2,1)S(1)} all-to-all(bf16[4,1,160,4608]{3,2,1,0:T(8,128)(2,1)S(1)} %stack.3), channel_id=1, replica_groups=mesh['node'=4,'hst'=32] {'node'}, dimensions={0} | all-to-all | bytes 11796480 | tf_op jit(solution)/shard_map/all_to_all | solution.py:48
  328.4 2.6 copy.9
Async XLA Ops:
  7.2 1.3 copy-start
  7.2 77.9 %reduce-scatter.2.cloned.1.call-start = ((), (), s32[]{:S(2)}) async-start(), calls=%async_computation.2 | async-start | bytes 7372800 | tf_op jit(solution)/shard_map/reduce_scatter | solution.py:33
  85.0 36.0 %copy-start.1 = (f32[1,160,4608]{2,1,0:T(8,128)S(1)}, f32[1,160,4608]{2,1,0:T(8,128)}, u32[]{:S(2)}) copy-start(f32[1,160,4608]{2,1,0:T(8,128)} %param.7) | copy-start | bytes 8847364
  85.0 36.0 %copy-start.2 = (bf16[160,4608]{1,0:T(8,128)(2,1)S(1)}, bf16[160,4608]{1,0:T(8,128)(2,1)}, u32[]{:S(2)}) copy-start(bf16[160,4608]{1,0:T(8,128)(2,1)} %reduce-scatter.2.cloned.1.call-done) | copy-start | bytes 4423684
  87.8 33.2 %collective-permute-start = (bf16[160,4608]{1,0:T(8,128)(2,1)S(1)}, bf16[160,4608]{1,0:T(8,128)(2,1)S(1)}, u32[]{:S(2)}, u32[]{:S(2)}) collective-permute-start(bf16[160,4608]{1,0:T(8,128)(2,1)S(1)} %fusion.6), channel_id=1, source_target_pairs={{0,1},{1,0},{2,3},{3,2},{4,5},{5,4},{6,7},{7,6},{8,9},{9,8},{10,11... | collective-permute-start | bytes 4423688 | tf_op jit(solution)/shard_map/ppermute | solution.py:18
  121.8 33.8 %collective-permute-start.1 = (bf16[160,4608]{1,0:T(8,128)(2,1)S(1)}, bf16[160,4608]{1,0:T(8,128)(2,1)S(1)}, u32[]{:S(2)}, u32[]{:S(2)}) collective-permute-start(bf16[160,4608]{1,0:T(8,128)(2,1)S(1)} %get-tuple-element.6), channel_id=1, source_target_pairs={{0,2},{2,0},{1,3},{3,1},{4,6},{6,4},{5,7},{7,5},{8,10},{10,8},{9,1... | collective-permute-start | bytes 4423688 | tf_op jit(solution)/shard_map/ppermute | solution.py:18
  156.0 31.4 %collective-permute-start.2 = (bf16[160,4608]{1,0:T(8,128)(2,1)S(1)}, bf16[160,4608]{1,0:T(8,128)(2,1)S(1)}, u32[]{:S(2)}, u32[]{:S(2)}) collective-permute-start(bf16[160,4608]{1,0:T(8,128)(2,1)S(1)} %fusion.7), channel_id=1, source_target_pairs={{0,4},{4,0},{1,5},{5,1},{2,6},{6,2},{3,7},{7,3},{8,12},{12,8},{9,1... | collective-permute-start | bytes 4423688 | tf_op jit(solution)/shard_map/ppermute | solution.py:18
  188.3 32.0 %collective-permute-start.3 = (bf16[160,4608]{1,0:T(8,128)(2,1)S(1)}, bf16[160,4608]{1,0:T(8,128)(2,1)S(1)}, u32[]{:S(2)}, u32[]{:S(2)}) collective-permute-start(bf16[160,4608]{1,0:T(8,128)(2,1)S(1)} %get-tuple-element.4), channel_id=1, source_target_pairs={{0,8},{8,0},{1,9},{9,1},{2,10},{10,2},{3,11},{11,3},{4,12},{12,4},... | collective-permute-start | bytes 4423688 | tf_op jit(solution)/shard_map/ppermute | solution.py:18
  220.2 30.0 %copy-start.3 = (f32[1,160,4608]{2,1,0:T(8,128)S(1)}, f32[1,160,4608]{2,1,0:T(8,128)}, u32[]{:S(2)}) copy-start(f32[1,160,4608]{2,1,0:T(8,128)} %param.8) | copy-start | bytes 8847364
  220.7 29.6 %collective-permute-start.4 = (bf16[160,4608]{1,0:T(8,128)(2,1)S(1)}, bf16[160,4608]{1,0:T(8,128)(2,1)S(1)}, u32[]{:S(2)}, u32[]{:S(2)}) collective-permute-start(bf16[160,4608]{1,0:T(8,128)(2,1)S(1)} %fusion.8), channel_id=1, source_target_pairs={{0,16},{16,0},{1,17},{17,1},{2,18},{18,2},{3,19},{19,3},{4,20},{20... | collective-permute-start | bytes 4423688 | tf_op jit(solution)/shard_map/ppermute | solution.py:18
Sparse Core Ops, SparseCore 0:
  19.1 65.8 reduce-scatter.1
